TPU v7x, 256 devices: a whole 4x4x8 slice. The times are simulated.
256 devices in a mesh: grp: 8 (over x, core), lx: 4 (over y), ly: 8 (over z).
Axes of the slice: x: 4, y: 4, z: 8, core: 2. Of those that a mesh axis runs over, the one named last changes fastest.
Arguments:
- vectors: float32 [32, 256, 4096], P('grp', 'lx', 'ly'), may hold values from -6 to 6
- levels: int32 [256, 4096], P('lx', 'ly'), may hold values from 0 to 7
- level_table: float32 [8], replicated, may hold values from 1 to 3
- filter_low: float32 [1], replicated, may hold values from -1 to 0.5
- filter_high: float32 [1], replicated, may hold values from 6 to 7.5
Outputs:
- basis: float32 [32, 256, 4096], P('grp', 'lx', 'ly')
All inputs are finite; a program needn't handle non-finite values.
Results may differ from a plain program's by a relative error of at most 0.00011.
Values sent between devices are 32-bit elements; how exact they have to be, the bound alone decides.
No kernel may reach another device: no remote copies, remote signals or barrier semaphores. Data moves between devices by JAX's collectives and lax.ppermute only.
A program may use at most 64 MiB of HBM per device.

v0:
```python
import jax
import jax.numpy as jnp
from jax import lax
from jax.sharding import PartitionSpec as P


def padded_2(shard, sides, width):
    for axis, dim in sides:
        size, length = (lax.axis_size(axis), shard.shape[dim])
        up = [(i, (i + 1) % size) for i in range(size)]
        down = [(j, i) for i, j in up]
        last = lax.slice_in_dim(shard, length - width, length, axis=dim)
        leading = lax.slice_in_dim(shard, 0, width, axis=dim)
        before = lax.ppermute(last, axis, up)
        after = lax.ppermute(leading, axis, down)
        shard = jnp.concatenate([before, shard, after], axis=dim)
    return shard


def from_root(value, axis, source):
    kept = jnp.where(lax.axis_index(axis) == source, value, 0).astype(value.dtype)
    return lax.psum(kept, axis)


def apply_operator(field, onsite):
    padded = padded_2(field, (("lx", 1), ("ly", 2)), 1)
    beside = padded[:, 2:, 1:-1] + padded[:, :-2, 1:-1] + padded[:, 1:-1, 2:] + padded[:, 1:-1, :-2]
    return onsite[None] * field - beside


def lower_inverse(gram):
    lower = jnp.linalg.cholesky(gram)
    eye_block = jnp.eye(gram.shape[0], dtype=jnp.float32)
    return lax.linalg.triangular_solve(lower, eye_block, left_side=True, lower=True)


def body(vectors, levels, level_table, filter_low, filter_high):
    count_vec, rows_local, cols_local = vectors.shape
    level_ids = jnp.arange(level_table.shape[0], dtype=jnp.int32)
    onsite = jnp.sum(
        jnp.where(levels[None] == level_ids[:, None, None], level_table[:, None, None], 0.0), axis=0
    )
    center = (filter_high[0] + filter_low[0]) / 2.0
    half = (filter_high[0] - filter_low[0]) / 2.0
    first = (apply_operator(vectors, onsite) - center * vectors) / half
    filtered = 2.0 * (apply_operator(first, onsite) - center * first) / half - vectors
    total = rows_local * cols_local * lax.axis_size("lx") * lax.axis_size("ly")
    flat = filtered.reshape(count_vec, rows_local * cols_local)
    highest = lax.Precision.HIGHEST
    mine = lax.axis_index("grp")
    result = jnp.zeros_like(flat)
    for h in range(lax.axis_size("grp")):
        gram = lax.psum(jnp.dot(flat, flat.T, precision=highest), ("lx", "ly")) / total
        done = jnp.dot(lower_inverse(gram), flat, precision=highest)
        result = jnp.where(mine == h, done, result)
        shared = from_root(done, "grp", h)
        coeff = lax.psum(jnp.dot(shared, flat.T, precision=highest), ("lx", "ly")) / total
        later = mine > h
        flat = jnp.where(later, flat - jnp.dot(coeff.T, shared, precision=highest), flat)
    return result.reshape(count_vec, rows_local, cols_local)


def solution(mesh):
    in_specs = (P("grp", "lx", "ly"), P("lx", "ly"), P(), P(), P())
    out_specs = P("grp", "lx", "ly")
    return jax.shard_map(body, mesh=mesh, in_specs=in_specs, out_specs=out_specs, check_vma=False)
```

profile of v0, /device:TPU:32, one launch (start us, length us, event | category | flops | bytes accessed | tf_op | source)
XLA Modules:
  0.0 1632.8 jit_solution(7607256732290742390)
XLA Ops:
  7.4 3.1 collective-permute-start
  11.9 3.5 collective-permute-done.1
  21.7 3.9 collective-permute-done.3
  26.2 2.0 collective-permute-start.5
  31.3 3.3 collective-permute-start.6
  34.6 2.7 collective-permute-done.6
  37.3 2.5 collective-permute-done.7
  40.2 2.4 convolution_bitcast_fusion
  42.6 71.0 %psum.154 = f32[4,4]{0,1:T(4,128)S(1)} all-reduce(f32[4,4]{0,1:T(4,128)S(1)} %convolution_bitcast_fusion), channel_id=1, replica_groups=mesh['grp'=8,'lx'=4,'ly'=8] {'lx','ly'}, use_global_device_ids=true, to_apply=%region_1.2 | all-reduce | flops 16 | bytes 128 | tf_op jit(solution)/shard_map/psum | solution.py:53
  118.3 60.3 %all-reduce.8.cloned.1.call-done = f32[4,32768]{1,0:T(4,128)} async-done(((f32[4,32768]{1,0:T(4,128)}), f32[4,32768]{1,0:T(4,128)}) %all-reduce.8.cloned.1.call-update) | async-done | bytes 524304 | tf_op jit(solution)/shard_map/psum | solution.py:22
  178.6 3.5 fusion.99
  182.1 71.6 %psum.156 = f32[4,4]{0,1:T(4,128)S(1)} all-reduce(f32[4,4]{0,1:T(4,128)S(1)} %fusion.99), channel_id=1, replica_groups=mesh['grp'=8,'lx'=4,'ly'=8] {'lx','ly'}, use_global_device_ids=true, to_apply=%region_5.8 | all-reduce | flops 16 | bytes 128 | tf_op jit(solution)/shard_map/psum | solution.py:57
  254.8 2.3 fusion.100
  257.1 73.6 %psum.157 = f32[4,4]{0,1:T(4,128)S(1)} all-reduce(f32[4,4]{0,1:T(4,128)S(1)} %fusion.100), channel_id=1, replica_groups=mesh['grp'=8,'lx'=4,'ly'=8] {'lx','ly'}, use_global_device_ids=true, to_apply=%region_6.9 | all-reduce | flops 16 | bytes 128 | tf_op jit(solution)/shard_map/psum | solution.py:53
  335.0 58.1 %all-reduce.10.cloned.1.call-done = f32[4,32768]{1,0:T(4,128)} async-done(((f32[4,32768]{1,0:T(4,128)}), f32[4,32768]{1,0:T(4,128)}) %all-reduce.10.cloned.1.call-update) | async-done | bytes 524304 | tf_op jit(solution)/shard_map/psum | solution.py:22
  393.1 3.5 fusion.101
  396.6 71.6 %psum.159 = f32[4,4]{0,1:T(4,128)S(1)} all-reduce(f32[4,4]{0,1:T(4,128)S(1)} %fusion.101), channel_id=1, replica_groups=mesh['grp'=8,'lx'=4,'ly'=8] {'lx','ly'}, use_global_device_ids=true, to_apply=%region_8.11 | all-reduce | flops 16 | bytes 128 | tf_op jit(solution)/shard_map/psum | solution.py:57
  469.2 2.3 fusion.102
  471.6 73.6 %psum.160 = f32[4,4]{0,1:T(4,128)S(1)} all-reduce(f32[4,4]{0,1:T(4,128)S(1)} %fusion.102), channel_id=1, replica_groups=mesh['grp'=8,'lx'=4,'ly'=8] {'lx','ly'}, use_global_device_ids=true, to_apply=%region_9.12 | all-reduce | flops 16 | bytes 128 | tf_op jit(solution)/shard_map/psum | solution.py:53
  549.8 57.8 %all-reduce.12.cloned.1.call-done = f32[4,32768]{1,0:T(4,128)} async-done(((f32[4,32768]{1,0:T(4,128)}), f32[4,32768]{1,0:T(4,128)}) %all-reduce.12.cloned.1.call-update) | async-done | bytes 524304 | tf_op jit(solution)/shard_map/psum | solution.py:22
  607.6 3.5 fusion.103
  611.1 71.6 %psum.162 = f32[4,4]{0,1:T(4,128)S(1)} all-reduce(f32[4,4]{0,1:T(4,128)S(1)} %fusion.103), channel_id=1, replica_groups=mesh['grp'=8,'lx'=4,'ly'=8] {'lx','ly'}, use_global_device_ids=true, to_apply=%region_11.14 | all-reduce | flops 16 | bytes 128 | tf_op jit(solution)/shard_map/psum | solution.py:57
  683.7 2.3 fusion.104
  686.1 73.6 %psum.163 = f32[4,4]{0,1:T(4,128)S(1)} all-reduce(f32[4,4]{0,1:T(4,128)S(1)} %fusion.104), channel_id=1, replica_groups=mesh['grp'=8,'lx'=4,'ly'=8] {'lx','ly'}, use_global_device_ids=true, to_apply=%region_12.15 | all-reduce | flops 16 | bytes 128 | tf_op jit(solution)/shard_map/psum | solution.py:53
  764.0 58.1 %all-reduce.14.cloned.1.call-done = f32[4,32768]{1,0:T(4,128)} async-done(((f32[4,32768]{1,0:T(4,128)}), f32[4,32768]{1,0:T(4,128)}) %all-reduce.14.cloned.1.call-update) | async-done | bytes 524304 | tf_op jit(solution)/shard_map/psum | solution.py:22
  822.1 3.5 fusion.105
  825.6 71.6 %psum.165 = f32[4,4]{0,1:T(4,128)S(1)} all-reduce(f32[4,4]{0,1:T(4,128)S(1)} %fusion.105), channel_id=1, replica_groups=mesh['grp'=8,'lx'=4,'ly'=8] {'lx','ly'}, use_global_device_ids=true, to_apply=%region_14.17 | all-reduce | flops 16 | bytes 128 | tf_op jit(solution)/shard_map/psum | solution.py:57
  898.2 2.3 fusion.106
  900.6 73.6 %psum.166 = f32[4,4]{0,1:T(4,128)S(1)} all-reduce(f32[4,4]{0,1:T(4,128)S(1)} %fusion.106), channel_id=1, replica_groups=mesh['grp'=8,'lx'=4,'ly'=8] {'lx','ly'}, use_global_device_ids=true, to_apply=%region_15.18 | all-reduce | flops 16 | bytes 128 | tf_op jit(solution)/shard_map/psum | solution.py:53
  978.9 57.6 %all-reduce.16.cloned.1.call-done = f32[4,32768]{1,0:T(4,128)} async-done(((f32[4,32768]{1,0:T(4,128)}), f32[4,32768]{1,0:T(4,128)}) %all-reduce.16.cloned.1.call-update) | async-done | bytes 524304 | tf_op jit(solution)/shard_map/psum | solution.py:22
  1036.6 3.5 fusion.107
  1040.0 71.6 %psum.168 = f32[4,4]{0,1:T(4,128)S(1)} all-reduce(f32[4,4]{0,1:T(4,128)S(1)} %fusion.107), channel_id=1, replica_groups=mesh['grp'=8,'lx'=4,'ly'=8] {'lx','ly'}, use_global_device_ids=true, to_apply=%region_17.20 | all-reduce | flops 16 | bytes 128 | tf_op jit(solution)/shard_map/psum | solution.py:57
  1111.6 2.0 fusion.2
  1113.7 2.3 fusion.108
  1116.0 73.6 %psum.169 = f32[4,4]{0,1:T(4,128)S(1)} all-reduce(f32[4,4]{0,1:T(4,128)S(1)} %fusion.108), channel_id=1, replica_groups=mesh['grp'=8,'lx'=4,'ly'=8] {'lx','ly'}, use_global_device_ids=true, to_apply=%region_18.21 | all-reduce | flops 16 | bytes 128 | tf_op jit(solution)/shard_map/psum | solution.py:53
  1192.1 2.0 broadcast_select_fusion.1
  1194.2 58.1 %all-reduce.18.cloned.1.call-done = f32[4,32768]{1,0:T(4,128)} async-done(((f32[4,32768]{1,0:T(4,128)}), f32[4,32768]{1,0:T(4,128)}) %all-reduce.18.cloned.1.call-update) | async-done | bytes 524304 | tf_op jit(solution)/shard_map/psum | solution.py:22
  1252.2 3.5 fusion.109
  1255.7 71.6 %psum.171 = f32[4,4]{0,1:T(4,128)S(1)} all-reduce(f32[4,4]{0,1:T(4,128)S(1)} %fusion.109), channel_id=1, replica_groups=mesh['grp'=8,'lx'=4,'ly'=8] {'lx','ly'}, use_global_device_ids=true, to_apply=%region_20.23 | all-reduce | flops 16 | bytes 128 | tf_op jit(solution)/shard_map/psum | solution.py:57
  1327.3 2.0 fusion.1
  1329.3 2.3 fusion.110
  1331.6 73.8 %psum.172 = f32[4,4]{0,1:T(4,128)S(1)} all-reduce(f32[4,4]{0,1:T(4,128)S(1)} %fusion.110), channel_id=1, replica_groups=mesh['grp'=8,'lx'=4,'ly'=8] {'lx','ly'}, use_global_device_ids=true, to_apply=%region_21.24 | all-reduce | flops 16 | bytes 128 | tf_op jit(solution)/shard_map/psum | solution.py:53
  1409.9 58.1 %all-reduce.20.cloned.1.call-done = f32[4,32768]{1,0:T(4,128)} async-done(((f32[4,32768]{1,0:T(4,128)}), f32[4,32768]{1,0:T(4,128)}) %all-reduce.20.cloned.1.call-update) | async-done | bytes 524304 | tf_op jit(solution)/shard_map/psum | solution.py:22
  1468.0 3.5 fusion.111
  1471.5 71.6 %psum.174 = f32[4,4]{0,1:T(4,128)S(1)} all-reduce(f32[4,4]{0,1:T(4,128)S(1)} %fusion.111), channel_id=1, replica_groups=mesh['grp'=8,'lx'=4,'ly'=8] {'lx','ly'}, use_global_device_ids=true, to_apply=%region_23.26 | all-reduce | flops 16 | bytes 128 | tf_op jit(solution)/shard_map/psum | solution.py:57
  1543.1 2.0 fusion
  1545.1 2.3 fusion.112
  1547.5 73.6 %psum.175 = f32[4,4]{0,1:T(4,128)S(1)} all-reduce(f32[4,4]{0,1:T(4,128)S(1)} %fusion.112), channel_id=1, replica_groups=mesh['grp'=8,'lx'=4,'ly'=8] {'lx','ly'}, use_global_device_ids=true, to_apply=%region_24.27 | all-reduce | flops 16 | bytes 128 | tf_op jit(solution)/shard_map/psum | solution.py:53
  (131 shorter events, 49.7 us)
Async XLA Ops:
  6.5 172.1 %all-reduce.8.cloned.1.call-start = ((), (), s32[]{:S(2)}) async-start(), calls=%async_computation | async-start | bytes 1048576 | tf_op jit(solution)/shard_map/psum | solution.py:22
  7.4 4.5 collective-permute-start
  10.5 8.1 copy-start.6
  10.5 15.1 copy-start
  10.5 4.9 collective-permute-start.1
  16.5 2.1 copy-start.7
  16.5 5.2 collective-permute-start.2
  16.7 9.0 collective-permute-start.3
  26.1 3.7 collective-permute-start.4
  26.2 4.9 collective-permute-start.5
  31.3 6.0 collective-permute-start.6
  34.6 5.1 collective-permute-start.7
  118.0 275.1 %all-reduce.10.cloned.1.call-start = ((), (), s32[]{:S(2)}) async-start(), calls=%async_computation.1 | async-start | bytes 1048576 | tf_op jit(solution)/shard_map/psum | solution.py:22
  178.6 75.1 %copy-start.5 = (f32[4,32768]{1,0:T(4,128)S(1)}, f32[4,32768]{1,0:T(4,128)}, u32[]{:S(2)}) copy-start(f32[4,32768]{1,0:T(4,128)} %all-reduce.8.cloned.1.call-done) | copy-start | bytes 1572868
  335.0 272.6 %all-reduce.12.cloned.1.call-start = ((), (), s32[]{:S(2)}) async-start(), calls=%async_computation.2 | async-start | bytes 1048576 | tf_op jit(solution)/shard_map/psum | solution.py:22
  393.1 75.1 %copy-start.2 = (f32[4,32768]{1,0:T(4,128)S(1)}, f32[4,32768]{1,0:T(4,128)}, u32[]{:S(2)}) copy-start(f32[4,32768]{1,0:T(4,128)} %all-reduce.10.cloned.1.call-done) | copy-start | bytes 1572868
  549.5 272.6 %all-reduce.14.cloned.1.call-start = ((), (), s32[]{:S(2)}) async-start(), calls=%async_computation.3 | async-start | bytes 1048576 | tf_op jit(solution)/shard_map/psum | solution.py:22
  607.6 75.1 %copy-start.3 = (f32[4,32768]{1,0:T(4,128)S(1)}, f32[4,32768]{1,0:T(4,128)}, u32[]{:S(2)}) copy-start(f32[4,32768]{1,0:T(4,128)} %all-reduce.12.cloned.1.call-done) | copy-start | bytes 1572868
  764.0 272.6 %all-reduce.16.cloned.1.call-start = ((), (), s32[]{:S(2)}) async-start(), calls=%async_computation.4 | async-start | bytes 1048576 | tf_op jit(solution)/shard_map/psum | solution.py:22
  822.1 75.1 %copy-start.4 = (f32[4,32768]{1,0:T(4,128)S(1)}, f32[4,32768]{1,0:T(4,128)}, u32[]{:S(2)}) copy-start(f32[4,32768]{1,0:T(4,128)} %all-reduce.14.cloned.1.call-done) | copy-start | bytes 1572868
  978.5 273.7 %all-reduce.18.cloned.1.call-start = ((), (), s32[]{:S(2)}) async-start(), calls=%async_computation.5 | async-start | bytes 1048576 | tf_op jit(solution)/shard_map/psum | solution.py:22
  1194.1 273.9 %all-reduce.20.cloned.1.call-start = ((), (), s32[]{:S(2)}) async-start(), calls=%async_computation.6 | async-start | bytes 1048576 | tf_op jit(solution)/shard_map/psum | solution.py:22
  1545.1 78.4 %copy-start.1 = (f32[4,32768]{1,0:T(4,128)S(1)}, f32[4,32768]{1,0:T(4,128)}, u32[]{:S(2)}) copy-start(f32[4,32768]{1,0:T(4,128)} %convolution_select_fusion.1) | copy-start | bytes 1572868
Sparse Core Ops, SparseCore 0:
  118.2 60.3 all-reduce.7
  335.1 57.9 all-reduce.9
  549.6 57.9 all-reduce.11
  764.1 57.9 all-reduce.13
  978.6 57.9 all-reduce.15
  1194.2 57.9 all-reduce.17
  1410.0 57.9 all-reduce.19
where the time goes:
time: 1640 us; the launch traced here: 1630 us
  blocking collectives  1090 us (66%)
  waiting for transfers between devices  427 us (26%)
  matrix products  69.2 us (4%)
  other arithmetic  19.4 us (1%)
    psum x8, blocking collectives, body(): lax.psum(jnp.dot(flat, flat.T, precision=highest), ('lx', 'ly')) / total  586 us
    psum x7, blocking collectives, body(): lax.psum(jnp.dot(shared, flat.T, precision=highest), ('lx', 'ly')) / total  501 us
    psum x7, waiting for transfers between devices, from_root(): return lax.psum(kept, axis)  408 us
  transfers between devices with their start and end apart: 15, of which 15 were waited for; matrix products, arithmetic and copies ran while one was open for 0% of the time, Pallas kernels for 0%

commit v1 on v0

--- a/solution.py
+++ b/solution.py
@@ -50,7 +50,12 @@
     mine = lax.axis_index("grp")
     result = jnp.zeros_like(flat)
     for h in range(lax.axis_size("grp")):
-        gram = lax.psum(jnp.dot(flat, flat.T, precision=highest), ("lx", "ly")) / total
+
+        def number_lane(chunk, across, mesh_dim):
+            w_next = lax.psum(lax.psum(chunk, across), mesh_dim)
+            return w_next
+
+        gram = number_lane(jnp.dot(flat, flat.T, precision=highest), "ly", "lx") / total
         done = jnp.dot(lower_inverse(gram), flat, precision=highest)
         result = jnp.where(mine == h, done, result)
         shared = from_root(done, "grp", h)

time: 1640 us -> 1270 us (0.77)
  blocking collectives: 1090 us -> 706 us
    psum x8 -> x16, blocking collectives: 586 us -> 205 us  [number_lane(): w_next = lax.psum(lax.psum(chunk, across), mesh_dim)]
where the time goes in v1:
time: 1270 us; the launch traced here: 1260 us
  blocking collectives  706 us (56%)
  waiting for transfers between devices  437 us (34%)
  matrix products  69.2 us (5%)
  other arithmetic  19.4 us (2%)
  between operations  15.3 us (1%)
    psum x7, blocking collectives, body(): lax.psum(jnp.dot(shared, flat.T, precision=highest), ('lx', 'ly')) / total  501 us
    psum x7, waiting for transfers between devices, from_root(): return lax.psum(kept, axis)  419 us
    psum x16, blocking collectives, number_lane(): w_next = lax.psum(lax.psum(chunk, across), mesh_dim)  205 us
  transfers between devices with their start and end apart: 15, of which 15 were waited for; matrix products, arithmetic and copies ran while one was open for 0% of the time, Pallas kernels for 0%

profile of v1, /device:TPU:32, one launch (start us, length us, event | category | flops | bytes accessed | tf_op | source)
XLA Modules:
  0.0 1262.1 jit_solution(12387116127768921658)
XLA Ops:
  7.4 3.1 collective-permute-start
  11.9 3.5 collective-permute-done.1
  21.7 3.9 collective-permute-done.3
  31.3 3.3 collective-permute-start.6
  34.6 2.7 collective-permute-done.6
  37.3 2.5 collective-permute-done.7
  40.2 2.4 convolution_bitcast_fusion
  42.6 15.4 %psum.210 = f32[4,4]{0,1:T(4,128)S(1)} all-reduce(f32[4,4]{0,1:T(4,128)S(1)} %convolution_bitcast_fusion), channel_id=1, replica_groups=mesh['grp'=8,'lx'=4,'ly'=8] {'ly'}, use_global_device_ids=true, to_apply=%region_1.2 | all-reduce | flops 16 | bytes 128 | tf_op jit(solution)/shard_map/psum | solution.py:55
  58.0 8.4 psum.211
  71.2 62.1 %all-reduce.8.cloned.1.call-done = f32[4,32768]{1,0:T(4,128)} async-done(((f32[4,32768]{1,0:T(4,128)}), f32[4,32768]{1,0:T(4,128)}) %all-reduce.8.cloned.1.call-update) | async-done | bytes 524304 | tf_op jit(solution)/shard_map/psum | solution.py:22
  133.3 3.5 fusion.99
  136.9 71.6 %psum.213 = f32[4,4]{0,1:T(4,128)S(1)} all-reduce(f32[4,4]{0,1:T(4,128)S(1)} %fusion.99), channel_id=1, replica_groups=mesh['grp'=8,'lx'=4,'ly'=8] {'lx','ly'}, use_global_device_ids=true, to_apply=%region_6.9 | all-reduce | flops 16 | bytes 128 | tf_op jit(solution)/shard_map/psum | solution.py:62
  209.5 2.3 fusion.100
  211.8 18.1 %psum.214 = f32[4,4]{0,1:T(4,128)S(1)} all-reduce(f32[4,4]{0,1:T(4,128)S(1)} %fusion.100), channel_id=1, replica_groups=mesh['grp'=8,'lx'=4,'ly'=8] {'ly'}, use_global_device_ids=true, to_apply=%region_7.10 | all-reduce | flops 16 | bytes 128 | tf_op jit(solution)/shard_map/psum | solution.py:55
  229.9 7.7 psum.215
  242.0 59.5 %all-reduce.10.cloned.1.call-done = f32[4,32768]{1,0:T(4,128)} async-done(((f32[4,32768]{1,0:T(4,128)}), f32[4,32768]{1,0:T(4,128)}) %all-reduce.10.cloned.1.call-update) | async-done | bytes 524304 | tf_op jit(solution)/shard_map/psum | solution.py:22
  301.6 3.5 fusion.101
  305.1 71.6 %psum.217 = f32[4,4]{0,1:T(4,128)S(1)} all-reduce(f32[4,4]{0,1:T(4,128)S(1)} %fusion.101), channel_id=1, replica_groups=mesh['grp'=8,'lx'=4,'ly'=8] {'lx','ly'}, use_global_device_ids=true, to_apply=%region_10.13 | all-reduce | flops 16 | bytes 128 | tf_op jit(solution)/shard_map/psum | solution.py:62
  380.0 18.1 %psum.218 = f32[4,4]{0,1:T(4,128)S(1)} all-reduce(f32[4,4]{0,1:T(4,128)S(1)} %fusion.102), channel_id=1, replica_groups=mesh['grp'=8,'lx'=4,'ly'=8] {'ly'}, use_global_device_ids=true, to_apply=%region_11.14 | all-reduce | flops 16 | bytes 128 | tf_op jit(solution)/shard_map/psum | solution.py:55
  398.1 7.7 psum.219
  410.5 59.3 %all-reduce.12.cloned.1.call-done = f32[4,32768]{1,0:T(4,128)} async-done(((f32[4,32768]{1,0:T(4,128)}), f32[4,32768]{1,0:T(4,128)}) %all-reduce.12.cloned.1.call-update) | async-done | bytes 524304 | tf_op jit(solution)/shard_map/psum | solution.py:22
  469.7 3.5 fusion.103
  473.3 71.6 %psum.221 = f32[4,4]{0,1:T(4,128)S(1)} all-reduce(f32[4,4]{0,1:T(4,128)S(1)} %fusion.103), channel_id=1, replica_groups=mesh['grp'=8,'lx'=4,'ly'=8] {'lx','ly'}, use_global_device_ids=true, to_apply=%region_14.17 | all-reduce | flops 16 | bytes 128 | tf_op jit(solution)/shard_map/psum | solution.py:62
  548.2 18.1 %psum.222 = f32[4,4]{0,1:T(4,128)S(1)} all-reduce(f32[4,4]{0,1:T(4,128)S(1)} %fusion.104), channel_id=1, replica_groups=mesh['grp'=8,'lx'=4,'ly'=8] {'ly'}, use_global_device_ids=true, to_apply=%region_15.18 | all-reduce | flops 16 | bytes 128 | tf_op jit(solution)/shard_map/psum | solution.py:55
  566.3 7.7 psum.223
  578.4 59.5 %all-reduce.14.cloned.1.call-done = f32[4,32768]{1,0:T(4,128)} async-done(((f32[4,32768]{1,0:T(4,128)}), f32[4,32768]{1,0:T(4,128)}) %all-reduce.14.cloned.1.call-update) | async-done | bytes 524304 | tf_op jit(solution)/shard_map/psum | solution.py:22
  637.9 3.5 fusion.105
  641.5 71.6 %psum.225 = f32[4,4]{0,1:T(4,128)S(1)} all-reduce(f32[4,4]{0,1:T(4,128)S(1)} %fusion.105), channel_id=1, replica_groups=mesh['grp'=8,'lx'=4,'ly'=8] {'lx','ly'}, use_global_device_ids=true, to_apply=%region_18.21 | all-reduce | flops 16 | bytes 128 | tf_op jit(solution)/shard_map/psum | solution.py:62
  714.1 2.3 fusion.106
  716.4 18.1 %psum.226 = f32[4,4]{0,1:T(4,128)S(1)} all-reduce(f32[4,4]{0,1:T(4,128)S(1)} %fusion.106), channel_id=1, replica_groups=mesh['grp'=8,'lx'=4,'ly'=8] {'ly'}, use_global_device_ids=true, to_apply=%region_19.22 | all-reduce | flops 16 | bytes 128 | tf_op jit(solution)/shard_map/psum | solution.py:55
  734.5 7.7 psum.227
  747.0 59.1 %all-reduce.16.cloned.1.call-done = f32[4,32768]{1,0:T(4,128)} async-done(((f32[4,32768]{1,0:T(4,128)}), f32[4,32768]{1,0:T(4,128)}) %all-reduce.16.cloned.1.call-update) | async-done | bytes 524304 | tf_op jit(solution)/shard_map/psum | solution.py:22
  806.1 3.5 fusion.107
  809.6 71.6 %psum.229 = f32[4,4]{0,1:T(4,128)S(1)} all-reduce(f32[4,4]{0,1:T(4,128)S(1)} %fusion.107), channel_id=1, replica_groups=mesh['grp'=8,'lx'=4,'ly'=8] {'lx','ly'}, use_global_device_ids=true, to_apply=%region_22.25 | all-reduce | flops 16 | bytes 128 | tf_op jit(solution)/shard_map/psum | solution.py:62
  883.2 2.3 fusion.108
  885.6 18.1 %psum.230 = f32[4,4]{0,1:T(4,128)S(1)} all-reduce(f32[4,4]{0,1:T(4,128)S(1)} %fusion.108), channel_id=1, replica_groups=mesh['grp'=8,'lx'=4,'ly'=8] {'ly'}, use_global_device_ids=true, to_apply=%region_23.26 | all-reduce | flops 16 | bytes 128 | tf_op jit(solution)/shard_map/psum | solution.py:55
  903.7 7.7 psum.231
  916.0 59.6 %all-reduce.18.cloned.1.call-done = f32[4,32768]{1,0:T(4,128)} async-done(((f32[4,32768]{1,0:T(4,128)}), f32[4,32768]{1,0:T(4,128)}) %all-reduce.18.cloned.1.call-update) | async-done | bytes 524304 | tf_op jit(solution)/shard_map/psum | solution.py:22
  975.5 3.5 fusion.109
  979.0 71.6 %psum.233 = f32[4,4]{0,1:T(4,128)S(1)} all-reduce(f32[4,4]{0,1:T(4,128)S(1)} %fusion.109), channel_id=1, replica_groups=mesh['grp'=8,'lx'=4,'ly'=8] {'lx','ly'}, use_global_device_ids=true, to_apply=%region_26.29 | all-reduce | flops 16 | bytes 128 | tf_op jit(solution)/shard_map/psum | solution.py:62
  1055.0 18.1 %psum.234 = f32[4,4]{0,1:T(4,128)S(1)} all-reduce(f32[4,4]{0,1:T(4,128)S(1)} %fusion.110), channel_id=1, replica_groups=mesh['grp'=8,'lx'=4,'ly'=8] {'ly'}, use_global_device_ids=true, to_apply=%region_27.30 | all-reduce | flops 16 | bytes 128 | tf_op jit(solution)/shard_map/psum | solution.py:55
  1073.1 7.9 psum.235
  1085.5 59.6 %all-reduce.20.cloned.1.call-done = f32[4,32768]{1,0:T(4,128)} async-done(((f32[4,32768]{1,0:T(4,128)}), f32[4,32768]{1,0:T(4,128)}) %all-reduce.20.cloned.1.call-update) | async-done | bytes 524304 | tf_op jit(solution)/shard_map/psum | solution.py:22
  1145.1 3.5 fusion.111
  1148.5 71.6 %psum.237 = f32[4,4]{0,1:T(4,128)S(1)} all-reduce(f32[4,4]{0,1:T(4,128)S(1)} %fusion.111), channel_id=1, replica_groups=mesh['grp'=8,'lx'=4,'ly'=8] {'lx','ly'}, use_global_device_ids=true, to_apply=%region_30.33 | all-reduce | flops 16 | bytes 128 | tf_op jit(solution)/shard_map/psum | solution.py:62
  1222.2 2.3 fusion.112
  1224.5 18.1 %psum.238 = f32[4,4]{0,1:T(4,128)S(1)} all-reduce(f32[4,4]{0,1:T(4,128)S(1)} %fusion.112), channel_id=1, replica_groups=mesh['grp'=8,'lx'=4,'ly'=8] {'ly'}, use_global_device_ids=true, to_apply=%region_31.34 | all-reduce | flops 16 | bytes 128 | tf_op jit(solution)/shard_map/psum | solution.py:55
  1242.6 7.7 psum.239
  (139 shorter events, 66.8 us)
Async XLA Ops:
  6.5 126.8 %all-reduce.8.cloned.1.call-start = ((), (), s32[]{:S(2)}) async-start(), calls=%async_computation | async-start | bytes 1048576 | tf_op jit(solution)/shard_map/psum | solution.py:22
  7.4 4.5 collective-permute-start
  10.5 8.1 copy-start.6
  10.5 15.1 %copy-start = (f32[4,64,512]{2,1,0:T(8,128)S(1)}, f32[4,64,512]{2,1,0:T(8,128)}, u32[]{:S(2)}) copy-start(f32[4,64,512]{2,1,0:T(8,128)} %param.8) | copy-start | bytes 1572868
  10.5 4.9 collective-permute-start.1
  16.5 2.1 copy-start.7
  16.5 5.2 collective-permute-start.2
  16.7 9.0 collective-permute-start.3
  26.1 3.7 collective-permute-start.4
  26.2 4.9 collective-permute-start.5
  31.3 6.0 collective-permute-start.6
  34.6 5.1 collective-permute-start.7
  71.0 230.6 %all-reduce.10.cloned.1.call-start = ((), (), s32[]{:S(2)}) async-start(), calls=%async_computation.1 | async-start | bytes 1048576 | tf_op jit(solution)/shard_map/psum | solution.py:22
  133.3 75.1 %copy-start.5 = (f32[4,32768]{1,0:T(4,128)S(1)}, f32[4,32768]{1,0:T(4,128)}, u32[]{:S(2)}) copy-start(f32[4,32768]{1,0:T(4,128)} %all-reduce.8.cloned.1.call-done) | copy-start | bytes 1572868
  242.0 227.8 %all-reduce.12.cloned.1.call-start = ((), (), s32[]{:S(2)}) async-start(), calls=%async_computation.2 | async-start | bytes 1048576 | tf_op jit(solution)/shard_map/psum | solution.py:22
  301.6 75.1 %copy-start.2 = (f32[4,32768]{1,0:T(4,128)S(1)}, f32[4,32768]{1,0:T(4,128)}, u32[]{:S(2)}) copy-start(f32[4,32768]{1,0:T(4,128)} %all-reduce.10.cloned.1.call-done) | copy-start | bytes 1572868
  410.2 227.8 %all-reduce.14.cloned.1.call-start = ((), (), s32[]{:S(2)}) async-start(), calls=%async_computation.3 | async-start | bytes 1048576 | tf_op jit(solution)/shard_map/psum | solution.py:22
  469.7 75.1 %copy-start.3 = (f32[4,32768]{1,0:T(4,128)S(1)}, f32[4,32768]{1,0:T(4,128)}, u32[]{:S(2)}) copy-start(f32[4,32768]{1,0:T(4,128)} %all-reduce.12.cloned.1.call-done) | copy-start | bytes 1572868
  578.4 227.8 %all-reduce.16.cloned.1.call-start = ((), (), s32[]{:S(2)}) async-start(), calls=%async_computation.4 | async-start | bytes 1048576 | tf_op jit(solution)/shard_map/psum | solution.py:22
  637.9 75.1 %copy-start.4 = (f32[4,32768]{1,0:T(4,128)S(1)}, f32[4,32768]{1,0:T(4,128)}, u32[]{:S(2)}) copy-start(f32[4,32768]{1,0:T(4,128)} %all-reduce.14.cloned.1.call-done) | copy-start | bytes 1572868
  746.6 228.9 %all-reduce.18.cloned.1.call-start = ((), (), s32[]{:S(2)}) async-start(), calls=%async_computation.5 | async-start | bytes 1048576 | tf_op jit(solution)/shard_map/psum | solution.py:22
  915.9 229.2 %all-reduce.20.cloned.1.call-start = ((), (), s32[]{:S(2)}) async-start(), calls=%async_computation.6 | async-start | bytes 1048576 | tf_op jit(solution)/shard_map/psum | solution.py:22
  1222.2 30.7 %copy-start.1 = (f32[4,32768]{1,0:T(4,128)S(1)}, f32[4,32768]{1,0:T(4,128)}, u32[]{:S(2)}) copy-start(f32[4,32768]{1,0:T(4,128)} %convolution_select_fusion.1) | copy-start | bytes 1572868
Sparse Core Ops, SparseCore 0:
  71.1 62.2 all-reduce.7
  242.1 59.3 all-reduce.9
  410.3 59.3 all-reduce.11
  578.5 59.3 all-reduce.13
  746.7 59.3 all-reduce.15
  916.0 59.4 all-reduce.17
  1085.6 59.4 all-reduce.19
